TPU v7x, 32 devices: a whole 2x2x4 slice. The times are simulated.
32 devices in a mesh: cp: 8 (over z, x), tp: 4 (over y, core).
Axes of the slice: x: 2, y: 2, z: 4, core: 2. Of those that a mesh axis runs over, the one named last changes fastest.
Arguments:
- tokens: bfloat16 [4096, 4096], P(('cp', 'tp')), may hold values from -6 to 6
- grad_out: bfloat16 [4096, 4096], P(('cp', 'tp')), may hold values from -6 to 6
- expert_ids: int32 [4096, 1], P(('cp', 'tp')), may hold values from 0 to 7; in each aligned block of 128 rows (0 to 127, 128 to 255, ...) at most 24 rows name the same one
- router_weights: float32 [4096, 1], P(('cp', 'tp')), may hold values from 0.2 to 1
- gate_weight: bfloat16 [8, 1536, 4096], P('cp', 'tp'), may hold values from -0.09375 to 0.09375
- up_weight: bfloat16 [8, 1536, 4096], P('cp', 'tp'), may hold values from -0.09375 to 0.09375
- down_weight: bfloat16 [8, 1536, 4096], P('cp', 'tp'), may hold values from -0.15625 to 0.15625
Outputs:
- grad_tokens: bfloat16 [4096, 4096], P(('cp', 'tp'))
- grad_gate: float32 [8, 1536, 4096], P('cp', 'tp')
- grad_up: float32 [8, 1536, 4096], P('cp', 'tp')
- grad_down: float32 [8, 1536, 4096], P('cp', 'tp')
Inputs may be any that keep to these rules, and one draw needn't show every extreme that they name: `expert_ids`: within each aligned block of 128 consecutive rows (rows 0 to 127, 128 to 255, and so on) each expert is named at most 24 times, and in some block some expert is named exactly 24 times.
All inputs are finite; a program needn't handle non-finite values.
Results may differ from a plain program's by a relative error of at most 0.009.
Values may be sent and summed in bfloat16 or wider, within the bound.
A program may use at most 256 MiB of HBM per device.

v0:
```python
import jax
import jax.numpy as jnp
from jax import lax
from jax.sharding import PartitionSpec as P


def expert_work(slot_in, slot_go, w_gate, w_up, w_down):
    rows_last = (((1,), (1,)), ((), ()))
    rows_first = (((0,), (0,)), ((), ()))
    gate = lax.dot_general(slot_in, w_gate, rows_last, preferred_element_type=jnp.float32)
    upval = lax.dot_general(slot_in, w_up, rows_last, preferred_element_type=jnp.float32)
    sig = jax.nn.sigmoid(gate)
    act = gate * sig
    hidden = (act * upval).astype(jnp.bfloat16)
    grad_hidden = lax.dot_general(slot_go, w_down, rows_last, preferred_element_type=jnp.float32)
    grad_upin = (grad_hidden * act).astype(jnp.bfloat16)
    grad_gatein = (grad_hidden * upval * sig * (1.0 + gate * (1.0 - sig))).astype(jnp.bfloat16)
    grad_down = lax.dot_general(hidden, slot_go, rows_first, preferred_element_type=jnp.float32)
    grad_gate = lax.dot_general(
        grad_gatein, slot_in, rows_first, preferred_element_type=jnp.float32
    )
    grad_up = lax.dot_general(grad_upin, slot_in, rows_first, preferred_element_type=jnp.float32)
    partial_value = jnp.dot(grad_gatein, w_gate, preferred_element_type=jnp.float32)
    partial_value = partial_value + jnp.dot(grad_upin, w_up, preferred_element_type=jnp.float32)
    return (partial_value, grad_gate, grad_up, grad_down)


def body(tokens, grad_out, expert_ids, router_weights, gate_weight, up_weight, down_weight):
    n_cp = lax.axis_size("cp")
    n_tp = lax.axis_size("tp")
    tok_rows, width = tokens.shape
    picks = expert_ids.shape[1]
    count = tok_rows * picks
    slots = max(2, 3 * tok_rows * picks // (2 * n_cp))
    flat_ids = expert_ids.reshape(count)
    onehot = (flat_ids[:, None] == jnp.arange(n_cp, dtype=jnp.int32)[None, :]).astype(jnp.int32)
    before = jnp.cumsum(onehot, axis=0) - onehot
    rank = jnp.sum(before * onehot, axis=1)
    place = flat_ids * slots + rank
    placer = (place[None, :] == jnp.arange(n_cp * slots, dtype=jnp.int32)[:, None]).astype(
        jnp.bfloat16
    )
    x_assign = jnp.repeat(tokens, picks, axis=0)
    g_assign = (router_weights * jnp.repeat(grad_out, picks, axis=0).astype(jnp.float32)).astype(
        jnp.bfloat16
    )
    x_slots = (
        jnp.dot(placer, x_assign, preferred_element_type=jnp.float32)
        .astype(jnp.bfloat16)
        .reshape(n_cp, slots, width)
    )
    g_slots = (
        jnp.dot(placer, g_assign, preferred_element_type=jnp.float32)
        .astype(jnp.bfloat16)
        .reshape(n_cp, slots, width)
    )
    w_gate = gate_weight[0]
    w_up = up_weight[0]
    w_down = down_weight[0]

    def spread(values):
        return jnp.broadcast_to(values[:, None], (n_cp, n_tp, slots, width)).reshape(
            n_cp * n_tp, slots, width
        )

    got_x, got_g = (
        lax.all_to_all(spread(x_slots), ("cp", "tp"), split_axis=0, concat_axis=0, tiled=True),
        lax.all_to_all(spread(g_slots), ("cp", "tp"), split_axis=0, concat_axis=0, tiled=True),
    )
    partial_value, grad_gate, grad_up, grad_down = expert_work(
        got_x.reshape(-1, width), got_g.reshape(-1, width), w_gate, w_up, w_down
    )
    sent = partial_value.astype(jnp.bfloat16).reshape(n_cp * n_tp, slots, width)
    back = lax.all_to_all(sent, ("cp", "tp"), split_axis=0, concat_axis=0, tiled=True)
    slot_grad = jnp.sum(back.reshape(n_cp, n_tp, slots, width).astype(jnp.float32), axis=1).astype(
        jnp.bfloat16
    )
    pick_grad = lax.dot_general(
        placer,
        slot_grad.reshape(n_cp * slots, width),
        (((0,), (0,)), ((), ())),
        preferred_element_type=jnp.float32,
    )
    grad_tokens = jnp.sum(pick_grad.reshape(tok_rows, picks, width), axis=1).astype(jnp.bfloat16)
    return (grad_tokens, grad_gate[None], grad_up[None], grad_down[None])


def solution(mesh):
    return jax.shard_map(
        body,
        mesh=mesh,
        in_specs=(
            P(("cp", "tp"), None),
            P(("cp", "tp"), None),
            P(("cp", "tp"), None),
            P(("cp", "tp"), None),
            P("cp", "tp", None),
            P("cp", "tp", None),
            P("cp", "tp", None),
        ),
        out_specs=(
            P(("cp", "tp"), None),
            P("cp", "tp", None),
            P("cp", "tp", None),
            P("cp", "tp", None),
        ),
        check_vma=False,
    )
```

profile of v0, /device:TPU:16, one launch (start us, length us, event | category | flops | bytes accessed | tf_op | source)
XLA Modules:
  0.0 470.4 jit_solution(6763455956814925385)
XLA Ops:
  0.6 0.0 copy-start
  0.6 0.9 fusion.12
  1.5 0.2 reduce_window_sum.11
  1.7 0.8 select_reduce_fusion
  2.5 0.7 multiply_add_fusion
  3.2 1.8 convolution_convert_fusion
  5.0 3.5 broadcast_in_dim.29
  8.5 0.0 copy-start.10
  8.5 6.0 %all-to-all-start.1 = ((bf16[32,24,4096]{2,1,0:T(8,128)(2,1)}), bf16[32,24,4096]{2,1,0:T(8,128)(2,1)}, u32[]{:S(2)}, u32[]{:S(2)}) async-start(bf16[32,24,4096]{2,1,0:T(8,128)(2,1)} %bitcast.48), calls=%async_computation.1 | async-start | bytes 12582912 | tf_op jit(solution)/shard_map/all_to_all | solution.py:67
  14.5 0.0 copy-done.10
  14.5 3.0 convolution_convert_fusion.1
  17.5 133.9 %all-to-all-done.1 = bf16[32,24,4096]{2,1,0:T(8,128)(2,1)} async-done(((bf16[32,24,4096]{2,1,0:T(8,128)(2,1)}), bf16[32,24,4096]{2,1,0:T(8,128)(2,1)}, u32[]{:S(2)}, u32[]{:S(2)}) %all-to-all-start.1) | async-done | bytes 6291488 | tf_op jit(solution)/shard_map/all_to_all | solution.py:67
  151.4 4.9 %broadcast_in_dim.27 = bf16[8,4,24,4096]{3,2,1,0:T(8,128)(2,1)} broadcast(bf16[8,24,4096]{2,1,0:T(8,128)(2,1)} %bitcast.49), dimensions={0,2,3} | broadcast | bytes 7864320 | tf_op jit(solution)/shard_map/broadcast_in_dim | solution.py:62
  156.3 8.8 %all-to-all-start = ((bf16[32,24,4096]{2,1,0:T(8,128)(2,1)}), bf16[32,24,4096]{2,1,0:T(8,128)(2,1)}, u32[]{:S(2)}, u32[]{:S(2)}) async-start(bf16[32,24,4096]{2,1,0:T(8,128)(2,1)} %bitcast.47), calls=%async_computation | async-start | bytes 12582912 | tf_op jit(solution)/shard_map/all_to_all | solution.py:68
  165.1 0.0 copy-done
  165.1 0.0 copy-start.4
  165.1 6.8 %fusion.2 = f32[768,384]{1,0:T(8,128)} fusion(bf16[768,4096]{1,0:T(8,128)(2,1)} %bitcast.8, bf16[1,384,4096]{2,1,0:T(8,128)(2,1)S(1)} %copy-done), kind=kOutput, calls=%fused_computation.10 | convolution fusion | flops 2415919104 | bytes 10616832 | tf_op jit(solution)/shard_map/dot_general | solution.py:10
  171.9 0.0 copy-done.4
  171.9 6.6 %fusion.5 = f32[768,384]{1,0:T(8,128)} fusion(bf16[768,4096]{1,0:T(8,128)(2,1)} %bitcast.8, bf16[1,384,4096]{2,1,0:T(8,128)(2,1)S(1)} %copy-done.4), kind=kOutput, calls=%fused_computation.13 | convolution fusion | flops 2415919104 | bytes 10616832 | tf_op jit(solution)/shard_map/dot_general | solution.py:11
  178.5 123.6 %all-to-all-done = bf16[32,24,4096]{2,1,0:T(8,128)(2,1)} async-done(((bf16[32,24,4096]{2,1,0:T(8,128)(2,1)}), bf16[32,24,4096]{2,1,0:T(8,128)(2,1)}, u32[]{:S(2)}, u32[]{:S(2)}) %all-to-all-start) | async-done | bytes 6291488 | tf_op jit(solution)/shard_map/all_to_all | solution.py:68
  302.1 8.1 %multiply_convert_fusion.2 = (bf16[768,384]{1,0:T(8,128)(2,1)S(1)}, bf16[768,384]{1,0:T(8,128)(2,1)S(1)}) fusion(f32[768,384]{1,0:T(8,128)} %fusion.2, f32[768,384]{1,0:T(8,128)} %fusion.5, bf16[768,4096]{1,0:T(8,128)(2,1)} %bitcast.4, bf16[1,384,4096]{2,1,0:T(8,128)(2,1)} %param.13), kind=kOutput, calls=%fused_computation.19 | convolution fusion | flops 2419752960 | bytes 12976128 | tf_op jit(solution)/shard_map/dot_general | solution.py:15
  310.2 0.0 copy-start.6
  310.2 0.0 copy-start.2
  310.2 0.0 copy-start.5
  310.2 3.5 fusion
  313.7 0.0 copy-done.6
  313.7 0.0 copy-done.2
  313.7 0.0 copy-done.5
  313.7 5.3 %add_convert_fusion = bf16[768,4096]{1,0:T(8,128)(2,1)} fusion(f32[768,4096]{1,0:T(8,128)S(1)} %fusion, bf16[768,384]{1,0:T(8,128)(2,1)S(1)} %get-tuple-element.4, bf16[1,384,4096]{2,1,0:T(8,128)(2,1)S(1)} %copy-done.5), kind=kOutput, calls=%fused_computation | convolution fusion | flops 2422210560 | bytes 22609920 | tf_op jit(solution)/shard_map/dot_general | solution.py:24
  319.0 0.0 copy-start.3
  319.0 8.8 %all-to-all-start.2 = ((bf16[32,24,4096]{2,1,0:T(8,128)(2,1)}), bf16[32,24,4096]{2,1,0:T(8,128)(2,1)}, u32[]{:S(2)}, u32[]{:S(2)}) async-start(bf16[32,24,4096]{2,1,0:T(8,128)(2,1)} %bitcast.46), calls=%async_computation.2 | async-start | bytes 12582912 | tf_op jit(solution)/shard_map/all_to_all | solution.py:74
  327.7 0.0 copy-done.3
  327.8 0.0 copy-start.7
  327.8 8.2 %convolution_bitcast_fusion.1 = f32[1,384,4096]{2,1,0:T(8,128)} fusion(bf16[768,384]{1,0:T(8,128)(2,1)S(1)} %copy-done.3, bf16[768,4096]{1,0:T(8,128)(2,1)} %bitcast.8), kind=kOutput, calls=%fused_computation.3 | convolution fusion | flops 2415919104 | bytes 13172736 | tf_op jit(solution)/shard_map/dot_general | solution.py:22
  336.0 0.0 copy-done.7
  336.0 0.0 copy-start.8
  336.0 0.0 copy-start.9
  336.0 8.3 %convolution_bitcast_fusion.2 = f32[1,384,4096]{2,1,0:T(8,128)} fusion(bf16[768,384]{1,0:T(8,128)(2,1)S(1)} %copy-done.7, bf16[768,4096]{1,0:T(8,128)(2,1)} %bitcast.8), kind=kOutput, calls=%fused_computation.4 | convolution fusion | flops 2415919104 | bytes 13172736 | tf_op jit(solution)/shard_map/dot_general | solution.py:19
  344.3 0.0 copy-done.8
  344.3 0.0 copy-done.9
  344.3 8.2 %convolution_bitcast_fusion = f32[1,384,4096]{2,1,0:T(8,128)} fusion(bf16[768,4096]{1,0:T(8,128)(2,1)} %bitcast.4, f32[768,384]{1,0:T(8,128)S(1)} %copy-done.9, f32[768,384]{1,0:T(8,128)S(1)} %copy-done.8), kind=kOutput, calls=%fused_computation.2 | convolution fusion | flops 2417688576 | bytes 14942208 | tf_op jit(solution)/shard_map/dot_general | solution.py:18
  352.5 112.2 %all-to-all-done.2 = bf16[32,24,4096]{2,1,0:T(8,128)(2,1)} async-done(((bf16[32,24,4096]{2,1,0:T(8,128)(2,1)}), bf16[32,24,4096]{2,1,0:T(8,128)(2,1)}, u32[]{:S(2)}, u32[]{:S(2)}) %all-to-all-start.2) | async-done | bytes 6291488 | tf_op jit(solution)/shard_map/all_to_all | solution.py:74
  464.7 0.0 copy-start.1
  464.7 4.2 bitcast_reduce_fusion
  468.9 1.5 convolution_convert_fusion.2
  470.4 0.0 copy-done.1
Async XLA Ops:
  0.6 164.5 %copy-start = (bf16[1,384,4096]{2,1,0:T(8,128)(2,1)S(1)}, bf16[1,384,4096]{2,1,0:T(8,128)(2,1)}, u32[]{:S(2)}) copy-start(bf16[1,384,4096]{2,1,0:T(8,128)(2,1)} %param.11) | copy-start | bytes 9437188
  8.5 6.0 %copy-start.10 = (f32[128,1]{0,1:T(1,128)S(1)}, f32[128,1]{0,1:T(1,128)}, u32[]{:S(2)}) copy-start(f32[128,1]{0,1:T(1,128)} %param.10) | copy-start | bytes 1540
  8.5 142.9 %all-to-all-start.1 = ((bf16[32,24,4096]{2,1,0:T(8,128)(2,1)}), bf16[32,24,4096]{2,1,0:T(8,128)(2,1)}, u32[]{:S(2)}, u32[]{:S(2)}) async-start(bf16[32,24,4096]{2,1,0:T(8,128)(2,1)} %bitcast.48), calls=%async_computation.1 | async-start | bytes 12582912 | tf_op jit(solution)/shard_map/all_to_all | solution.py:67
  156.3 145.7 %all-to-all-start = ((bf16[32,24,4096]{2,1,0:T(8,128)(2,1)}), bf16[32,24,4096]{2,1,0:T(8,128)(2,1)}, u32[]{:S(2)}, u32[]{:S(2)}) async-start(bf16[32,24,4096]{2,1,0:T(8,128)(2,1)} %bitcast.47), calls=%async_computation | async-start | bytes 12582912 | tf_op jit(solution)/shard_map/all_to_all | solution.py:68
  165.1 6.8 %copy-start.4 = (bf16[1,384,4096]{2,1,0:T(8,128)(2,1)S(1)}, bf16[1,384,4096]{2,1,0:T(8,128)(2,1)}, u32[]{:S(2)}) copy-start(bf16[1,384,4096]{2,1,0:T(8,128)(2,1)} %param.12) | copy-start | bytes 9437188
  310.2 3.5 copy-start.6
  310.2 3.5 copy-start.2
  310.2 3.5 copy-start.5
  319.0 8.8 %copy-start.3 = (bf16[768,384]{1,0:T(8,128)(2,1)S(1)}, bf16[768,384]{1,0:T(8,128)(2,1)}, u32[]{:S(2)}) copy-start(bf16[768,384]{1,0:T(8,128)(2,1)} %copy-done.2) | copy-start | bytes 1769476
  319.0 145.7 %all-to-all-start.2 = ((bf16[32,24,4096]{2,1,0:T(8,128)(2,1)}), bf16[32,24,4096]{2,1,0:T(8,128)(2,1)}, u32[]{:S(2)}, u32[]{:S(2)}) async-start(bf16[32,24,4096]{2,1,0:T(8,128)(2,1)} %bitcast.46), calls=%async_computation.2 | async-start | bytes 12582912 | tf_op jit(solution)/shard_map/all_to_all | solution.py:74
  327.8 8.2 %copy-start.7 = (bf16[768,384]{1,0:T(8,128)(2,1)S(1)}, bf16[768,384]{1,0:T(8,128)(2,1)}, u32[]{:S(2)}) copy-start(bf16[768,384]{1,0:T(8,128)(2,1)} %copy-done.6) | copy-start | bytes 1769476
  336.0 8.3 %copy-start.8 = (f32[768,384]{1,0:T(8,128)S(1)}, f32[768,384]{1,0:T(8,128)}, u32[]{:S(2)}) copy-start(f32[768,384]{1,0:T(8,128)} %fusion.2) | copy-start | bytes 3538948
  336.0 8.3 %copy-start.9 = (f32[768,384]{1,0:T(8,128)S(1)}, f32[768,384]{1,0:T(8,128)}, u32[]{:S(2)}) copy-start(f32[768,384]{1,0:T(8,128)} %fusion.5) | copy-start | bytes 3538948
  464.7 5.7 %copy-start.1 = (bf16[1,384,4096]{2,1,0:T(8,128)(2,1)S(1)}, bf16[1,384,4096]{2,1,0:T(8,128)(2,1)}, u32[]{:S(2)}) copy-start(bf16[1,384,4096]{2,1,0:T(8,128)(2,1)} %param.11) | copy-start | bytes 9437188
where the time goes:
time: 475 us; the launch traced here: 470 us
  waiting for transfers between devices  370 us (78%)
  matrix products  61.1 us (13%)
  starting transfers between devices  23.5 us (5%)
  local copies, waits for them, and re-layouts  8.43 us (2%)
  other arithmetic  6.76 us (1%)
    all_to_all x1, waiting for transfers between devices, body(): lax.all_to_all(spread(x_slots), ('cp', 'tp'), split_axis=0, concat_axis=0...  134 us
    all_to_all x1, waiting for transfers between devices, body(): lax.all_to_all(spread(g_slots), ('cp', 'tp'), split_axis=0, concat_axis=0...  124 us
    all_to_all x1, waiting for transfers between devices, body(): lax.all_to_all(sent, ('cp', 'tp'), split_axis=0, concat_axis=0, tiled=True)  112 us
  transfers between devices with their start and end apart: 3, of which 3 were waited for; matrix products, arithmetic and copies ran while one was open for 9% of the time, Pallas kernels for 0%

commit v1 on v0

v1 whole, which is shorter than its diff:
```python
import functools

import jax
import jax.numpy as jnp
from jax import lax
from jax.experimental import pallas as pl
from jax.experimental.pallas import tpu as pltpu
from jax.sharding import PartitionSpec as P

F32 = jnp.float32
BF16 = jnp.bfloat16
ROWS_LAST = (((1,), (1,)), ((), ()))
ROWS_FIRST = (((0,), (0,)), ((), ()))


def flip(c, d, n):
    total, b = 0, 1
    while b < n:
        bit = (c // b) % 2
        total = total + ((1 - bit) if d & b else bit) * b
        b *= 2
    return total


def positions(n_tp):
    c = lax.axis_index("cp")
    t = lax.axis_index("tp")
    n_y = n_tp // 2
    k = t % 2
    y = t // 2
    return c, t, n_y, k, y


def greet(n_cp, n_tp):
    c, t, n_y, k, y = positions(n_tp)
    barrier = pltpu.get_barrier_semaphore()
    peers = [(flip(c, d, n_cp), t) for d in range(1, n_cp)]
    peers += [(c, ((y + dy) % n_y) * 2 + k) for dy in range(1, n_y)]
    peers += [(c, y * 2 + 1 - k)]
    for peer in peers:
        pl.semaphore_signal(barrier, inc=1, device_id=peer, device_id_type=pl.DeviceIdType.MESH)
    pl.semaphore_wait(barrier, len(peers))


def remote(src, dst, send, recv, peer):
    return pltpu.make_async_remote_copy(
        src_ref=src, dst_ref=dst, send_sem=send, recv_sem=recv,
        device_id=peer, device_id_type=pl.DeviceIdType.MESH,
    )


def send_order(n_cp):
    far = list(range(n_cp // 2, n_cp))
    near = list(range(1, n_cp // 2))
    out = []
    for i, f in enumerate(far):
        out.append(f)
        if i < len(near):
            out.append(near[i])
    return out


def dispatch_kernel(n_cp, n_tp, xg, out, loc, cp_s, cp_r, y_s, y_r, s_s, s_r, f_s, f_r):
    c, t, n_y, k, y = positions(n_tp)
    sib = y * 2 + 1 - k
    greet(n_cp, n_tp)

    def cell(s, tt):
        return out.at[:, s * n_tp + tt]

    def cp_copy(d):
        peer = flip(c, d, n_cp)
        return remote(xg.at[:, peer], cell(c, t), cp_s.at[d], cp_r.at[d], (peer, t))

    def have(d):
        return xg.at[:, c] if d == 0 else cell(flip(c, d, n_cp), t)

    def y_copy(d, dy):
        to = ((y + dy) % n_y) * 2 + k
        return remote(have(d), cell(flip(c, d, n_cp), t), y_s.at[d, dy], y_r.at[d, dy], (c, to))

    def s_copy(d):
        return remote(have(d), cell(flip(c, d, n_cp), t), s_s.at[d], s_r.at[d], (c, sib))

    def f_copy(d, dy):
        part = cell(flip(c, d, n_cp), ((y + n_y - dy) % n_y) * 2 + k)
        return remote(part, part, f_s.at[d, dy], f_r.at[d, dy], (c, sib))

    own = pltpu.make_async_copy(xg.at[:, c], cell(c, t), loc)
    own.start()
    for d in send_order(n_cp):
        cp_copy(d).start()
    order = list(range(n_cp))
    for i in range(n_cp + 1):
        if i < n_cp:
            d = order[i]
            if d:
                cp_copy(d).wait_recv()
            for dy in range(1, n_y):
                y_copy(d, dy).start()
            s_copy(d).start()
        if i > 0:
            d = order[i - 1]
            for dy in range(1, n_y):
                y_copy(d, dy).wait_recv()
                f_copy(d, dy).start()
    own.wait()
    for d in range(n_cp):
        if d:
            cp_copy(d).wait_send()
        for dy in range(1, n_y):
            y_copy(d, dy).wait_send()
            f_copy(d, dy).wait()
        s_copy(d).wait()


def return_kernel(n_cp, n_tp, p, out, a, sb, yb, tb, loc, s_s, s_r, y_s, y_r, cp_s, cp_r):
    c, t, n_y, k, y = positions(n_tp)
    sib = y * 2 + 1 - k
    greet(n_cp, n_tp)
    order = list(range(n_cp // 2, n_cp)) + list(range(n_cp // 2))

    def s_copy(d, yy):
        s = flip(c, d, n_cp)
        return remote(
            p.at[s * n_tp + yy * 2 + 1 - k], a.at[d * n_y + yy],
            s_s.at[d, yy], s_r.at[d, yy], (c, sib),
        )

    def y_copy(d, dy):
        to = ((y + dy) % n_y) * 2 + k
        return remote(sb.at[d, dy], yb.at[d, dy], y_s.at[d, dy], y_r.at[d, dy], (c, to))

    def cp_copy(d):
        peer = flip(c, d, n_cp)
        return remote(tb.at[d], out.at[c], cp_s.at[d], cp_r.at[d], (peer, t))

    def pair(d, yy):
        s = flip(c, d, n_cp)
        return p[s * n_tp + yy * 2 + k].astype(F32) + a[d * n_y + yy].astype(F32)

    for d in order:
        for yy in range(n_y):
            s_copy(d, yy).start()
    own = pltpu.make_async_copy(tb.at[0], out.at[c], loc)
    for i in range(n_cp + 1):
        if i < n_cp:
            d = order[i]
            for yy in range(n_y):
                s_copy(d, yy).wait_recv()
            for dy in range(1, n_y):
                sb[d, dy] = pair(d, (y + dy) % n_y).astype(BF16)
                y_copy(d, dy).start()
        if i > 0:
            d = order[i - 1]
            total = pair(d, y)
            for dy in range(1, n_y):
                y_copy(d, dy).wait_recv()
                total = total + yb[d, dy].astype(F32)
            tb[d] = total.astype(BF16)
            if d:
                cp_copy(d).start()
            else:
                own.start()
    own.wait()
    for d in range(n_cp):
        for yy in range(n_y):
            s_copy(d, yy).wait_send()
        for dy in range(1, n_y):
            y_copy(d, dy).wait_send()
        if d:
            cp_copy(d).wait()


def dispatch(xg, n_cp, n_tp):
    _, _, slots, width = xg.shape
    n_y = n_tp // 2
    dma = pltpu.SemaphoreType.DMA
    return pl.pallas_call(
        functools.partial(dispatch_kernel, n_cp, n_tp),
        out_shape=jax.ShapeDtypeStruct((2, n_cp * n_tp, slots, width), BF16),
        in_specs=[pl.BlockSpec(memory_space=pl.ANY)],
        out_specs=pl.BlockSpec(memory_space=pl.ANY),
        scratch_shapes=[
            dma, dma((n_cp,)), dma((n_cp,)), dma((n_cp, n_y)), dma((n_cp, n_y)),
            dma((n_cp,)), dma((n_cp,)), dma((n_cp, n_y)), dma((n_cp, n_y)),
        ],
        compiler_params=pltpu.CompilerParams(collective_id=0, has_side_effects=True),
        name="dispatch",
    )(xg)


def give_back(p, n_cp, n_tp):
    _, slots, width = p.shape
    n_y = n_tp // 2
    dma = pltpu.SemaphoreType.DMA
    return pl.pallas_call(
        functools.partial(return_kernel, n_cp, n_tp),
        out_shape=jax.ShapeDtypeStruct((n_cp, slots, width), BF16),
        in_specs=[pl.BlockSpec(memory_space=pltpu.VMEM)],
        out_specs=pl.BlockSpec(memory_space=pltpu.VMEM),
        scratch_shapes=[
            pltpu.VMEM((n_cp * n_y, slots, width), BF16),
            pltpu.VMEM((n_cp, n_y, slots, width), BF16),
            pltpu.VMEM((n_cp, n_y, slots, width), BF16),
            pltpu.VMEM((n_cp, slots, width), BF16),
            dma, dma((n_cp, n_y)), dma((n_cp, n_y)), dma((n_cp, n_y)), dma((n_cp, n_y)),
            dma((n_cp,)), dma((n_cp,)),
        ],
        compiler_params=pltpu.CompilerParams(
            collective_id=1, has_side_effects=True, vmem_limit_bytes=56 << 20
        ),
        name="give_back",
    )(p)


def body(tokens, grad_out, expert_ids, router_weights, gate_weight, up_weight, down_weight):
    n_cp = lax.axis_size("cp")
    n_tp = lax.axis_size("tp")
    tok_rows, width = tokens.shape
    picks = expert_ids.shape[1]
    count = tok_rows * picks
    slots = -(-max(2, 3 * tok_rows * picks // (2 * n_cp)) // 8) * 8
    flat_ids = expert_ids.reshape(count)
    onehot = (flat_ids[:, None] == jnp.arange(n_cp, dtype=jnp.int32)[None, :]).astype(jnp.int32)
    before = jnp.cumsum(onehot, axis=0) - onehot
    rank = jnp.sum(before * onehot, axis=1)
    place = flat_ids * slots + rank
    placer = (place[None, :] == jnp.arange(n_cp * slots, dtype=jnp.int32)[:, None]).astype(BF16)
    x_assign = jnp.repeat(tokens, picks, axis=0)
    g_assign = (router_weights.reshape(count, 1) * jnp.repeat(grad_out, picks, axis=0).astype(F32)).astype(BF16)
    xg = jnp.stack([
        jnp.dot(placer, x_assign, preferred_element_type=F32).astype(BF16),
        jnp.dot(placer, g_assign, preferred_element_type=F32).astype(BF16),
    ]).reshape(2, n_cp, slots, width)
    w_gate = gate_weight[0]
    w_up = up_weight[0]
    w_down = down_weight[0]
    got = dispatch(xg, n_cp, n_tp).reshape(2, n_cp * n_tp * slots, width)
    slot_in, slot_go = got[0], got[1]
    gate = lax.dot_general(slot_in, w_gate, ROWS_LAST, preferred_element_type=F32)
    upval = lax.dot_general(slot_in, w_up, ROWS_LAST, preferred_element_type=F32)
    sig = jax.nn.sigmoid(gate)
    act = gate * sig
    hidden = (act * upval).astype(BF16)
    grad_hidden = lax.dot_general(slot_go, w_down, ROWS_LAST, preferred_element_type=F32)
    grad_upin = (grad_hidden * act).astype(BF16)
    grad_gatein = (grad_hidden * upval * sig * (1.0 + gate * (1.0 - sig))).astype(BF16)
    part = jnp.dot(grad_gatein, w_gate, preferred_element_type=F32)
    part = part + jnp.dot(grad_upin, w_up, preferred_element_type=F32)
    slot_grad = give_back(part.astype(BF16).reshape(n_cp * n_tp, slots, width), n_cp, n_tp)
    grad_down = lax.dot_general(hidden, slot_go, ROWS_FIRST, preferred_element_type=F32)
    grad_gate = lax.dot_general(grad_gatein, slot_in, ROWS_FIRST, preferred_element_type=F32)
    grad_up = lax.dot_general(grad_upin, slot_in, ROWS_FIRST, preferred_element_type=F32)
    pick_grad = lax.dot_general(
        placer, slot_grad.reshape(n_cp * slots, width), ROWS_FIRST, preferred_element_type=F32
    )
    grad_tokens = jnp.sum(pick_grad.reshape(tok_rows, picks, width), axis=1).astype(BF16)
    return (grad_tokens, grad_gate[None], grad_up[None], grad_down[None])


def solution(mesh):
    tok = P(("cp", "tp"), None)
    wgt = P("cp", "tp", None)
    return jax.shard_map(
        body,
        mesh=mesh,
        in_specs=(tok, tok, tok, tok, wgt, wgt, wgt),
        out_specs=(tok, wgt, wgt, wgt),
        check_vma=False,
    )
```

time: 475 us -> 203 us (0.43)
  waiting for transfers between devices: 370 us -> 0 us
  Pallas kernels: 0 us -> 148 us
  starting transfers between devices: 23.5 us -> 0 us
  matrix products: 61.1 us -> 42.6 us
    all_to_all x3 -> x0, waiting for transfers between devices: 370 us -> none  [the longest x1 134 us: body(): lax.all_to_all(spread(x_slots), ('cp', 'tp'), split_axis=0, concat_axis=0...]
    pallas_call x0 -> x2, Pallas kernels: none -> 148 us  [the longest x1 93.2 us: dispatch(): pl.pallas_call(functools.partial(dispatch_kernel, n_cp, n_tp), out_shape=...]
    all_to_all x3 -> x0, starting transfers between devices: 23.5 us -> none  [the longest x1 8.78 us: body(): lax.all_to_all(spread(g_slots), ('cp', 'tp'), split_axis=0, concat_axis=0...]
    dot_general x11, matrix products: 61.1 us -> 42.6 us  [the longest x1 8.67 us: body(): part = part + jnp.dot(grad_upin, w_up, preferred_element_type=F32)]
    broadcast_in_dim x2 -> x0, local copies, waits for them, and re-layouts: 8.37 us -> none  [spread(): jnp.broadcast_to(values[:, None], (n_cp, n_tp, slots, width))]
    slice x0 -> x1, local copies, waits for them, and re-layouts: none -> 5.76 us  [body(): slot_in, slot_go = (got[0], got[1])]
  transfers between devices with their start and end apart: 3 -> 0, of which waited for: 3 -> 0; matrix products, arithmetic and copies ran while one was open for 9% -> 0% of each run, Pallas kernels for 0% -> 0%
where the time goes in v1:
time: 203 us
  Pallas kernels  148 us (73%)
  matrix products  42.6 us (21%)
  local copies, waits for them, and re-layouts  6.64 us (3%)
  other arithmetic  4.58 us (2%)
    pallas_call x1, Pallas kernels, dispatch(): pl.pallas_call(functools.partial(dispatch_kernel, n_cp, n_tp), out_shape=...  93.2 us
    pallas_call x1, Pallas kernels, give_back(): pl.pallas_call(functools.partial(return_kernel, n_cp, n_tp), out_shape=ja...  54.6 us
    dot_general x1, matrix products, body(): part = part + jnp.dot(grad_upin, w_up, preferred_element_type=F32)  8.67 us
    slice x1, local copies, waits for them, and re-layouts, body(): slot_in, slot_go = (got[0], got[1])  5.76 us
    dot_general x1, matrix products, body(): lax.dot_general(hidden, slot_go, ROWS_FIRST, preferred_element_type=F32)  4.63 us
    dot_general x1, matrix products, body(): lax.dot_general(slot_go, w_down, ROWS_LAST, preferred_element_type=F32)  4.61 us
    dot_general x1, matrix products, body(): lax.dot_general(grad_upin, slot_in, ROWS_FIRST, preferred_element_type=F32)  4.55 us
    dot_general x1, matrix products, body(): lax.dot_general(grad_gatein, slot_in, ROWS_FIRST, preferred_element_type=...  4.53 us

profile of v1, /device:TPU:16, one launch (start us, length us, event | category | flops | bytes accessed | tf_op | source)
XLA Modules:
  0.0 202.5 jit_solution(1193995489794718810)
XLA Ops:
  0.6 0.0 copy-start
  0.6 0.9 fusion.12
  1.5 0.2 reduce_window_sum.11
  1.7 0.0 copy-start.12
  1.7 0.9 select_reduce_fusion
  2.6 0.7 multiply_add_fusion
  3.3 1.9 convolution_convert_fusion
  5.2 0.0 copy-done.12
  5.2 0.6 convolution_convert_fusion.1
  5.8 1.9 pad_maximum_fusion.xg
  7.7 93.2 %dispatch.1 = bf16[2,32,24,4096]{3,2,1,0:T(8,128)(2,1)} custom-call(bf16[2,8,24,4096]{3,2,1,0:T(8,128)(2,1)} %pad_maximum_fusion.xg), custom_call_target="tpu_custom_call" | custom-call | tf_op jit(solution)/shard_map/dispatch/pallas_call | solution.py:179
  100.9 5.8 %fusion.17 = (bf16[1,32,24,4096]{3,2,1,0:T(8,128)(2,1)S(1)}, bf16[1,32,24,4096]{3,2,1,0:T(8,128)(2,1)S(1)}) fusion(bf16[2,32,24,4096]{3,2,1,0:T(8,128)(2,1)} %dispatch.1), kind=kLoop, calls=%fused_computation.33 | loop fusion | bytes 25165824 | tf_op jit(solution)/shard_map/slice | solution.py:240
  106.7 0.0 copy-start.2
  106.7 0.0 copy-start.3
  106.7 0.0 copy-done
  106.7 0.0 copy-start.5
  106.7 3.4 %fusion.2 = f32[768,384]{1,0:T(8,128)S(1)} fusion(bf16[768,4096]{1,0:T(8,128)(2,1)S(1)} %bitcast.42, bf16[1,384,4096]{2,1,0:T(8,128)(2,1)S(1)} %copy-done), kind=kOutput, calls=%fused_computation.10 | convolution fusion | flops 2415919104 | bytes 10616832 | tf_op jit(solution)/shard_map/dot_general | solution.py:241
  110.2 0.0 copy-done.2
  110.2 0.8 copy-done.5
  111.0 0.0 copy-start.8
  111.0 3.4 %fusion.5 = f32[768,384]{1,0:T(8,128)S(1)} fusion(bf16[768,4096]{1,0:T(8,128)(2,1)S(1)} %bitcast.43, bf16[1,384,4096]{2,1,0:T(8,128)(2,1)S(1)} %copy-done.5), kind=kOutput, calls=%fused_computation.13 | convolution fusion | flops 2415919104 | bytes 10616832 | tf_op jit(solution)/shard_map/dot_general | solution.py:242
  114.4 0.0 copy-start.10
  114.4 0.0 copy-done.3
  114.4 0.0 copy-done.8
  114.4 0.0 copy-done.13
  114.4 4.6 %multiply_convert_fusion.2 = (bf16[768,384]{1,0:T(8,128)(2,1)}, bf16[768,384]{1,0:T(8,128)(2,1)S(1)}) fusion(f32[768,384]{1,0:T(8,128)S(1)} %fusion.2, f32[768,384]{1,0:T(8,128)S(1)} %fusion.5, bf16[768,4096]{1,0:T(8,128)(2,1)S(1)} %bitcast.49, bf16[1,384,4096]{2,1,0:T(8,128)(2,1)S(1)} %copy-done.13), kind=kOutput, calls=%fused_computation.19 | convolution fusion | flops 2419752960 | bytes 12976128 | tf_op jit(solution)/shard_map/dot_general | solution.py:246
  119.1 0.0 copy-done.10
  119.1 3.5 %fusion = f32[768,4096]{1,0:T(8,128)S(1)} fusion(bf16[768,384]{1,0:T(8,128)(2,1)S(1)} %get-tuple-element.7, bf16[1,384,4096]{2,1,0:T(8,128)(2,1)S(1)} %copy-done), kind=kOutput, calls=%fused_computation.8 | convolution fusion | flops 2415919104 | bytes 16318464 | tf_op jit(solution)/shard_map/dot_general | solution.py:249
  122.5 0.0 copy-done.6
  122.5 0.0 slice-start.1
  122.5 8.7 %add_convert_fusion = bf16[768,4096]{1,0:T(8,128)(2,1)} fusion(f32[768,4096]{1,0:T(8,128)S(1)} %fusion, bf16[768,384]{1,0:T(8,128)(2,1)} %get-tuple-element.6, bf16[1,384,4096]{2,1,0:T(8,128)(2,1)} %param.12), kind=kOutput, calls=%fused_computation | convolution fusion | flops 2422210560 | bytes 22609920 | tf_op jit(solution)/shard_map/dot_general | solution.py:250
  131.2 54.6 %give_back.1 = bf16[8,24,4096]{2,1,0:T(8,128)(2,1)} custom-call(bf16[32,24,4096]{2,1,0:T(8,128)(2,1)} %bitcast.48), custom_call_target="tpu_custom_call" | custom-call | tf_op jit(solution)/shard_map/give_back/pallas_call | solution.py:197
  185.8 2.9 %convolution_convert_fusion.2 = bf16[128,4096]{1,0:T(8,128)(2,1)} fusion(bf16[192,4096]{1,0:T(8,128)(2,1)} %bitcast.55, s32[128]{0:T(128)S(1)} %multiply_add_fusion), kind=kOutput, calls=%fused_computation.6 | convolution fusion | flops 201875456 | bytes 2621952 | tf_op jit(solution)/shard_map/dot_general | solution.py:255
  188.7 0.0 slice-done
  188.7 0.0 slice-done.1
  188.7 0.0 copy-done.7
  188.7 0.0 copy-start.4
  188.7 0.0 slice-start.2
  188.7 4.5 %convolution_bitcast_fusion.2 = f32[1,384,4096]{2,1,0:T(8,128)} fusion(bf16[768,384]{1,0:T(8,128)(2,1)S(1)} %copy-done.7, bf16[768,4096]{1,0:T(8,128)(2,1)S(1)} %bitcast.46), kind=kOutput, calls=%fused_computation.3 | convolution fusion | flops 2415919104 | bytes 13172736 | tf_op jit(solution)/shard_map/dot_general | solution.py:253
  193.3 0.0 copy-done.4
  193.3 4.5 %convolution_bitcast_fusion.1 = f32[1,384,4096]{2,1,0:T(8,128)} fusion(bf16[768,384]{1,0:T(8,128)(2,1)S(1)} %copy-done.4, bf16[768,4096]{1,0:T(8,128)(2,1)S(1)} %bitcast.47), kind=kOutput, calls=%fused_computation.2 | convolution fusion | flops 2415919104 | bytes 13172736 | tf_op jit(solution)/shard_map/dot_general | solution.py:254
  197.8 0.0 slice-done.2
  197.8 0.0 slice-done.3
  197.8 0.0 copy-done.9
  197.8 0.0 copy-done.11
  197.9 0.0 copy-start.1
  197.9 4.6 %convolution_bitcast_fusion = f32[1,384,4096]{2,1,0:T(8,128)} fusion(bf16[768,4096]{1,0:T(8,128)(2,1)S(1)} %bitcast.52, f32[768,384]{1,0:T(8,128)S(1)} %copy-done.11, f32[768,384]{1,0:T(8,128)S(1)} %copy-done.9), kind=kOutput, calls=%fused_computation.1 | convolution fusion | flops 2417688576 | bytes 14942208 | tf_op jit(solution)/shard_map/dot_general | solution.py:252
  202.5 0.0 copy-done.1
  (9 shorter events, 0.0 us)
Async XLA Ops:
  0.6 106.1 %copy-start = (bf16[1,384,4096]{2,1,0:T(8,128)(2,1)S(1)}, bf16[1,384,4096]{2,1,0:T(8,128)(2,1)}, u32[]{:S(2)}) copy-start(bf16[1,384,4096]{2,1,0:T(8,128)(2,1)} %param.11) | copy-start | bytes 9437188
  1.7 3.5 %copy-start.12 = (bf16[128,4096]{1,0:T(8,128)(2,1)S(1)}, bf16[128,4096]{1,0:T(8,128)(2,1)}, u32[]{:S(2)}) copy-start(bf16[128,4096]{1,0:T(8,128)(2,1)} %param.7) | copy-start | bytes 3145732
  106.7 3.5 %copy-start.2 = (bf16[1,32,24,4096]{3,2,1,0:T(8,128)(2,1)}, bf16[1,32,24,4096]{3,2,1,0:T(8,128)(2,1)S(1)}, u32[]{:S(2)}) copy-start(bf16[1,32,24,4096]{3,2,1,0:T(8,128)(2,1)S(1)} %get-tuple-element.5) | copy-start | bytes 18874372
  106.7 7.7 %copy-start.3 = (bf16[1,32,24,4096]{3,2,1,0:T(8,128)(2,1)}, bf16[1,32,24,4096]{3,2,1,0:T(8,128)(2,1)S(1)}, u32[]{:S(2)}) copy-start(bf16[1,32,24,4096]{3,2,1,0:T(8,128)(2,1)S(1)} %get-tuple-element.4) | copy-start | bytes 18874372
  106.7 4.2 %copy-start.5 = (bf16[1,384,4096]{2,1,0:T(8,128)(2,1)S(1)}, bf16[1,384,4096]{2,1,0:T(8,128)(2,1)}, u32[]{:S(2)}) copy-start(bf16[1,384,4096]{2,1,0:T(8,128)(2,1)} %param.12) | copy-start | bytes 9437188
  111.0 3.5 %copy-start.8 = (f32[768,384]{1,0:T(8,128)}, f32[768,384]{1,0:T(8,128)S(1)}, u32[]{:S(2)}) copy-start(f32[768,384]{1,0:T(8,128)S(1)} %fusion.2) | copy-start | bytes 3538948
  111.0 3.5 %copy-start.13 = (bf16[1,384,4096]{2,1,0:T(8,128)(2,1)S(1)}, bf16[1,384,4096]{2,1,0:T(8,128)(2,1)}, u32[]{:S(2)}) copy-start(bf16[1,384,4096]{2,1,0:T(8,128)(2,1)} %param.13) | copy-start | bytes 9437188
  114.4 4.7 %copy-start.10 = (f32[768,384]{1,0:T(8,128)}, f32[768,384]{1,0:T(8,128)S(1)}, u32[]{:S(2)}) copy-start(f32[768,384]{1,0:T(8,128)S(1)} %fusion.5) | copy-start | bytes 3538948
  119.1 3.5 %copy-start.6 = (bf16[768,384]{1,0:T(8,128)(2,1)}, bf16[768,384]{1,0:T(8,128)(2,1)S(1)}, u32[]{:S(2)}) copy-start(bf16[768,384]{1,0:T(8,128)(2,1)S(1)} %get-tuple-element.7) | copy-start | bytes 1769476
  119.1 69.6 %slice-start = ((s8[6291456]{0:T(1024)(128)(4,1)}), s8[4194304]{0:T(1024)(128)(4,1)S(1)}, s32[]{:S(2)}) async-start(s8[6291456]{0:T(1024)(128)(4,1)} %bitcast.44), calls=%async_computation | async-start | bytes 8388608
  122.5 66.2 %slice-start.1 = ((s8[6291456]{0:T(1024)(128)(4,1)}), s8[2097152]{0:T(1024)(128)(4,1)S(1)}, s32[]{:S(2)}) async-start(s8[6291456]{0:T(1024)(128)(4,1)} %bitcast.44), calls=%async_computation.1 | async-start | bytes 4194304
  131.2 57.5 %copy-start.7 = (bf16[768,384]{1,0:T(8,128)(2,1)S(1)}, bf16[768,384]{1,0:T(8,128)(2,1)}, u32[]{:S(2)}) copy-start(bf16[768,384]{1,0:T(8,128)(2,1)} %copy-done.6) | copy-start | bytes 1769476
  188.7 4.5 %copy-start.4 = (bf16[768,384]{1,0:T(8,128)(2,1)S(1)}, bf16[768,384]{1,0:T(8,128)(2,1)}, u32[]{:S(2)}) copy-start(bf16[768,384]{1,0:T(8,128)(2,1)} %get-tuple-element.6) | copy-start | bytes 1769476
  188.7 9.1 %slice-start.2 = ((s8[6291456]{0:T(1024)(128)(4,1)}), s8[4194304]{0:T(1024)(128)(4,1)S(1)}, s32[]{:S(2)}) async-start(s8[6291456]{0:T(1024)(128)(4,1)} %bitcast.50), calls=%async_computation.2 | async-start | bytes 8388608
  193.3 4.6 %slice-start.3 = ((s8[6291456]{0:T(1024)(128)(4,1)}), s8[2097152]{0:T(1024)(128)(4,1)S(1)}, s32[]{:S(2)}) async-start(s8[6291456]{0:T(1024)(128)(4,1)} %bitcast.50), calls=%async_computation.3 | async-start | bytes 4194304
  193.3 4.6 %copy-start.9 = (f32[768,384]{1,0:T(8,128)S(1)}, f32[768,384]{1,0:T(8,128)}, u32[]{:S(2)}) copy-start(f32[768,384]{1,0:T(8,128)} %copy-done.8) | copy-start | bytes 3538948
  193.3 4.6 %copy-start.11 = (f32[768,384]{1,0:T(8,128)S(1)}, f32[768,384]{1,0:T(8,128)}, u32[]{:S(2)}) copy-start(f32[768,384]{1,0:T(8,128)} %copy-done.10) | copy-start | bytes 3538948
  197.9 4.6 %copy-start.1 = (bf16[1,384,4096]{2,1,0:T(8,128)(2,1)S(1)}, bf16[1,384,4096]{2,1,0:T(8,128)(2,1)}, u32[]{:S(2)}) copy-start(bf16[1,384,4096]{2,1,0:T(8,128)(2,1)} %param.11) | copy-start | bytes 9437188
